TPU v7x, 32 devices: a whole 2x2x4 slice. The times are simulated.
32 devices in a mesh: dp: 8 (over z, x), expert: 4 (over y, core).
Axes of the slice: x: 2, y: 2, z: 4, core: 2. Of those that a mesh axis runs over, the one named last changes fastest.
Arguments:
- tokens: bfloat16 [4096, 2048], P(('dp', 'expert')), may hold values from -6 to 6
- d_out: bfloat16 [4096, 2048], P(('dp', 'expert')), may hold values from -6 to 6
- routes: int32 [4096, 2], P(('dp', 'expert')), may hold values from 0 to 3, all different within a row; in each aligned block of 128 rows (0 to 127, 128 to 255, ...) at most 96 rows name the same one
- gate_fixed: int32 [4096, 2], P(('dp', 'expert')), may hold values from 1 to 65535
- w_gate: bfloat16 [4, 2048, 768], P('expert'), may hold values from -0.125 to 0.125
- w_up: bfloat16 [4, 2048, 768], P('expert'), may hold values from -0.125 to 0.125
- w_down: bfloat16 [4, 768, 2048], P('expert'), may hold values from -0.21875 to 0.21875
Outputs:
- d_tokens: bfloat16 [4096, 2048], P(('dp', 'expert'))
- d_wgate: float32 [4, 2048, 768], P('expert', 'dp')
- d_wup: float32 [4, 2048, 768], P('expert', 'dp')
- d_wdown: float32 [4, 768, 2048], P('expert', 'dp')
Inputs may be any that keep to these rules, and one draw needn't show every extreme that they name: Each token names 2 different experts; of the routes of one device's 128 tokens (aligned blocks of rows) at most 96 name any one expert, a bound that some block reaches of them.
All inputs are finite; a program needn't handle non-finite values.
Results may differ from a plain program's by a relative error of at most 0.0065.
Values may be sent and summed in bfloat16 or wider, within the bound.
A program may use at most 192 MiB of HBM per device.

v0:
```python
import jax
import jax.numpy as jnp
from jax import lax
from jax.sharding import PartitionSpec as P


def forward_part(rows_x, w_gate, w_up):
    pre_gate = jnp.einsum("erd,edi->eri", rows_x, w_gate, preferred_element_type=jnp.float32)
    pre_up = jnp.einsum("erd,edi->eri", rows_x, w_up, preferred_element_type=jnp.float32)
    return (pre_gate, pre_up)


def backward_part(pre_gate, pre_up, scaled, w_gate, w_up, w_down):
    sigmoid_gate = jax.nn.sigmoid(pre_gate)
    silu_gate = pre_gate * sigmoid_gate
    hidden = (silu_gate * pre_up).astype(jnp.bfloat16)
    d_hidden = jnp.einsum("erd,eid->eri", scaled, w_down, preferred_element_type=jnp.float32)
    d_gate = (d_hidden * pre_up * sigmoid_gate * (1.0 + pre_gate * (1.0 - sigmoid_gate))).astype(
        jnp.bfloat16
    )
    d_up = (d_hidden * silu_gate).astype(jnp.bfloat16)
    route_grad = (
        jnp.einsum("eri,edi->erd", d_gate, w_gate, preferred_element_type=jnp.float32)
        + jnp.einsum("eri,edi->erd", d_up, w_up, preferred_element_type=jnp.float32)
    ).astype(jnp.bfloat16)
    return (hidden, d_gate, d_up, route_grad)


def body(tokens, d_out, routes, gate_fixed, w_gate, w_up, w_down):
    expert_span = lax.axis_size("expert")
    replicas = lax.axis_size("dp")
    local_count = w_gate.shape[0]
    expert_total = expert_span * local_count
    token_count, top_count = routes.shape
    model_width = tokens.shape[1]
    hidden_units = w_gate.shape[2]
    capacity = 3 * token_count * top_count // (2 * expert_total)
    inverse = 1.0 / replicas
    expert_ids = routes.reshape(-1)
    one_hot = (expert_ids[:, None] == jnp.arange(expert_total, dtype=jnp.int32)[None, :]).astype(
        jnp.int32
    )
    earlier = jnp.cumsum(one_hot, axis=0) - one_hot
    slot_index = jnp.sum(earlier * one_hot, axis=1)
    target = expert_ids * capacity + slot_index
    placing = (
        target[:, None] == jnp.arange(expert_total * capacity, dtype=jnp.int32)[None, :]
    ).astype(jnp.bfloat16)
    token_placing = jnp.sum(placing.reshape(token_count, top_count, -1), axis=1)
    gate_value = gate_fixed.astype(jnp.float32) / 65536.0
    scaled_routes = (gate_value[:, :, None] * d_out[:, None, :].astype(jnp.float32)).astype(
        jnp.bfloat16
    )
    scaled_routes = scaled_routes.reshape(-1, model_width)
    send_x = jnp.einsum("ts,td->sd", token_placing, tokens, preferred_element_type=jnp.float32)
    send_x = send_x.astype(jnp.bfloat16).reshape(expert_total, capacity, model_width)
    send_scaled = jnp.einsum(
        "rs,rd->sd", placing, scaled_routes, preferred_element_type=jnp.float32
    )
    send_scaled = send_scaled.astype(jnp.bfloat16).reshape(expert_total, capacity, model_width)
    rows_x, scaled = (
        lax.all_to_all(send_x, "expert", split_axis=0, concat_axis=1, tiled=True),
        lax.all_to_all(send_scaled, "expert", split_axis=0, concat_axis=1, tiled=True),
    )
    pre_gate, pre_up = forward_part(rows_x, w_gate, w_up)
    hidden, d_gate, d_up, route_grad = backward_part(pre_gate, pre_up, scaled, w_gate, w_up, w_down)
    returned = lax.all_to_all(route_grad, "expert", split_axis=1, concat_axis=0, tiled=True)
    route_rows = jnp.einsum(
        "rs,sd->rd", placing, returned.reshape(-1, model_width), preferred_element_type=jnp.float32
    )
    d_tokens = jnp.sum(route_rows.reshape(token_count, top_count, model_width), axis=1).astype(
        jnp.bfloat16
    )
    stacked = jnp.concatenate([d_gate, d_up], axis=2)
    feature_rows = model_width // replicas
    split_rows = rows_x.reshape(local_count, rows_x.shape[1], replicas, feature_rows)
    columns = lax.all_to_all(split_rows, "dp", split_axis=2, concat_axis=1, tiled=True)
    columns = columns.reshape(local_count, -1, feature_rows)
    reduced = (
        jnp.einsum(
            "erc,erj->cej",
            columns,
            lax.all_gather(stacked, "dp", axis=1, tiled=True),
            preferred_element_type=jnp.float32,
        )
        * inverse
    )
    d_wgate = jnp.transpose(reduced[:, :, :hidden_units], (1, 0, 2))
    d_wup = jnp.transpose(reduced[:, :, hidden_units:], (1, 0, 2))
    down_reduced = lax.psum_scatter(
        jnp.einsum("erc,erd->ced", hidden, scaled, preferred_element_type=jnp.float32) * inverse,
        "dp",
        scatter_dimension=0,
        tiled=True,
    )
    d_wdown = jnp.transpose(down_reduced, (1, 0, 2))
    return (d_tokens, d_wgate, d_wup, d_wdown)


def solution(mesh):
    in_specs = (
        P(("dp", "expert"), None),
        P(("dp", "expert"), None),
        P(("dp", "expert"), None),
        P(("dp", "expert"), None),
        P("expert", None, None),
        P("expert", None, None),
        P("expert", None, None),
    )
    out_specs = (
        P(("dp", "expert"), None),
        P("expert", "dp", None),
        P("expert", "dp", None),
        P("expert", "dp", None),
    )
    return jax.shard_map(body, mesh=mesh, in_specs=in_specs, out_specs=out_specs, check_vma=False)
```

profile of v0, /device:TPU:0, one launch (start us, length us, event | category | flops | bytes accessed | tf_op | source)
XLA Modules:
  0.0 478.5 jit_solution(15510985037377215370)
XLA Ops:
  7.2 0.0 copy-start
  7.2 0.9 copy.83
  8.1 0.1 eq.71
  8.3 0.1 eq.67
  8.4 1.2 reduce-window.6
  9.6 0.1 slice.16
  9.7 0.1 copy.85
  9.9 0.1 copy.86
  10.0 0.1 add_bitcast_fusion
  10.1 0.1 reduce_sum.33
  10.2 0.1 copy.87
  10.3 0.7 multiply_add_fusion.1
  11.0 0.1 fusion.35
  11.1 2.8 convolution_convert_fusion
  13.9 4.4 all-to-all-start.1
  18.3 3.4 mul.95
  21.7 3.7 mul.96
  25.4 0.0 copy-done.5
  25.4 0.1 copy.88
  25.5 0.1 mul.93
  25.7 3.4 convolution_convert_fusion.1
  29.1 10.0 %all-to-all-done.1 = bf16[4,96,2048]{2,1,0:T(8,128)(2,1)} async-done(((bf16[4,96,2048]{2,1,0:T(8,128)(2,1)}), bf16[4,96,2048]{2,1,0:T(8,128)(2,1)}, u32[]{:S(2)}, u32[]{:S(2)}) %all-to-all-start.1) | async-done | bytes 1572896 | tf_op jit(solution)/shard_map/all_to_all | solution.py:62
  39.0 4.4 all-to-all-start
  43.4 0.0 all-reduce.3.cloned.1.call-start
  43.5 0.0 copy-start.6
  43.5 4.1 fusion.4
  47.6 3.8 fusion.8
  51.4 12.2 %all-to-all-done = bf16[4,96,2048]{2,1,0:T(8,128)(2,1)} async-done(((bf16[4,96,2048]{2,1,0:T(8,128)(2,1)}), bf16[4,96,2048]{2,1,0:T(8,128)(2,1)}, u32[]{:S(2)}, u32[]{:S(2)}) %all-to-all-start) | async-done | bytes 1572896 | tf_op jit(solution)/shard_map/all_to_all | solution.py:63
  63.6 6.7 %multiply_bitcast_fusion = f32[768,1,2048]{0,2,1:T(8,128)} fusion(bf16[384,2048]{1,0:T(8,128)(2,1)} %bitcast.4, f32[384,768]{1,0:T(8,128)} %fusion.8, f32[384,768]{1,0:T(8,128)} %fusion.4), kind=kOutput, calls=%fused_computation.2 | convolution fusion | flops 1211301888 | bytes 10223616 | tf_op jit(solution)/shard_map/erc,erd->ced/dot_general | solution.py:91
  70.2 15.9 %copy.91 = f32[768,1,2048]{2,1,0:T(1,128)} copy(f32[768,1,2048]{0,2,1:T(8,128)} %multiply_bitcast_fusion) | data formatting | bytes 12582912 | tf_op jit(solution)/shard_map/mul | solution.py:91
  86.2 0.0 all-reduce.3.cloned.1.call-update
  86.2 0.2 all-gather.2.cloned.1.call-start
  86.4 4.7 multiply_convert_fusion.2
  91.2 0.0 copy-start.2
  91.2 0.0 copy-start.4
  91.2 0.8 copy-done.2
  92.0 0.2 copy-done.4
  92.2 1.1 pad_maximum_fusion
  93.3 0.0 all-gather.2.cloned.1.call-update
  93.3 0.0 copy-start.3
  93.3 0.0 copy-start.7
  93.3 2.6 fusion.2
  96.0 1.4 fusion.20
  97.4 2.4 copy.106
  99.9 0.5 broadcast.74
  100.4 11.3 %reduce.1 = bf16[384,2048]{1,0:T(8,128)(2,1)} reduce(bf16[384,1,2048]{2,1,0:T(2,128)(2,1)S(1)} %bitcast.98, bf16[]{:T(256)} %broadcast.74), dimensions={1}, to_apply=%bitcast.97.reduce_sub_computation | reduce | bytes 3145730
  111.7 4.2 reshape.180
  115.9 3.6 all-to-all-start.2
  119.4 1.9 copy.97
  121.4 1.5 copy.90
  122.8 16.7 %all-to-all-done.2 = bf16[4,2,98304]{2,1,0:T(2,128)(2,1)S(1)} async-done(((bf16[4,2,98304]{2,1,0:T(2,128)(2,1)}), bf16[4,2,98304]{2,1,0:T(2,128)(2,1)S(1)}, u32[]{:S(2)}, u32[]{:S(2)}) %all-to-all-start.2) | async-done | bytes 1572896 | tf_op jit(solution)/shard_map/all_to_all | solution.py:67
  139.5 6.6 %all-to-all-start.3 = ((bf16[1,384,8,256]{3,1,0,2:T(8,128)(2,1)}), bf16[1,384,8,256]{3,1,0,2:T(8,128)(2,1)}, u32[]{:S(2)}, u32[]{:S(2)}) async-start(bf16[1,384,8,256]{3,1,0,2:T(8,128)(2,1)} %copy.90), calls=%async_computation.3 | async-start | bytes 3145728 | tf_op jit(solution)/shard_map/all_to_all | solution.py:77
  146.1 0.6 dynamic-slice
  147.3 2.9 reshape.181
  150.2 4.0 fusion.26
  154.2 166.2 %all-reduce.3.cloned.1.call-done = f32[768,1,2048]{2,1,0:T(1,128)} async-done(((f32[768,1,2048]{2,1,0:T(1,128)}), f32[768,1,2048]{2,1,0:T(1,128)}) %all-reduce.3.cloned.1.call-update) | async-done | bytes 6291472
  320.5 1.2 dynamic-slice_bitcast_fusion
  321.7 1.1 copy.94
  322.8 0.0 all-to-all-done.3
  322.8 137.2 %all-gather.2.cloned.1.call-done = bf16[1,3072,1536]{2,1,0:T(8,128)(2,1)} async-done(((bf16[1,384,1536]{2,1,0:T(8,128)(2,1)}), bf16[1,3072,1536]{2,1,0:T(8,128)(2,1)}) %all-gather.2.cloned.1.call-update) | async-done | bytes 9437200 | tf_op jit(solution)/shard_map/all_gather | solution.py:83
  460.0 5.7 %fusion.17 = f32[256,1,1536]{0,2,1:T(8,128)S(1)} fusion(bf16[3072,256]{1,0:T(8,128)(2,1)} %bitcast.16, bf16[1,3072,1536]{2,1,0:T(8,128)(2,1)} %all-gather.2.cloned.1.call-done), kind=kOutput, calls=%fused_computation.17 | convolution fusion | flops 2416312320 | bytes 12582912 | tf_op jit(solution)/shard_map/erc,erj->cej/dot_general | solution.py:80
  465.7 1.2 slice_bitcast_fusion
  466.9 2.4 copy.92
  469.4 2.3 copy.93
  (15 shorter events, 0.1 us)
Async XLA Ops:
  7.2 36.3 %copy-start = (bf16[1,2048,768]{2,1,0:T(8,128)(2,1)S(1)}, bf16[1,2048,768]{2,1,0:T(8,128)(2,1)}, u32[]{:S(2)}) copy-start(bf16[1,2048,768]{2,1,0:T(8,128)(2,1)} %param.11) | copy-start | bytes 9437188
  13.9 25.1 %all-to-all-start.1 = ((bf16[4,96,2048]{2,1,0:T(8,128)(2,1)}), bf16[4,96,2048]{2,1,0:T(8,128)(2,1)}, u32[]{:S(2)}, u32[]{:S(2)}) async-start(bf16[4,96,2048]{2,1,0:T(8,128)(2,1)} %bitcast.99), calls=%async_computation.1 | async-start | bytes 3145728 | tf_op jit(solution)/shard_map/all_to_all | solution.py:62
  21.7 3.7 copy-start.5
  39.0 24.5 %all-to-all-start = ((bf16[4,96,2048]{2,1,0:T(8,128)(2,1)}), bf16[4,96,2048]{2,1,0:T(8,128)(2,1)}, u32[]{:S(2)}, u32[]{:S(2)}) async-start(bf16[4,96,2048]{2,1,0:T(8,128)(2,1)} %bitcast.100), calls=%async_computation | async-start | bytes 3145728 | tf_op jit(solution)/shard_map/all_to_all | solution.py:63
  43.4 277.1 %all-reduce.3.cloned.1.call-start = ((), (), s32[]{:S(2)}) async-start(), calls=%async_computation.5 | async-start | bytes 12582912
  43.5 4.1 copy-start.6
  86.2 373.8 %all-gather.2.cloned.1.call-start = ((), (), s32[]{:S(2)}) async-start(), calls=%async_computation.4 | async-start | bytes 10616832 | tf_op jit(solution)/shard_map/all_gather | solution.py:83
  91.2 0.8 copy-start.2
  91.2 1.0 copy-start.4
  93.3 2.7 copy-start.3
  93.3 2.7 copy-start.7
  115.9 23.6 %all-to-all-start.2 = ((bf16[4,2,98304]{2,1,0:T(2,128)(2,1)}), bf16[4,2,98304]{2,1,0:T(2,128)(2,1)S(1)}, u32[]{:S(2)}, u32[]{:S(2)}) async-start(bf16[4,2,98304]{2,1,0:T(2,128)(2,1)} %reshape.180), calls=%async_computation.2 | async-start | bytes 3145728 | tf_op jit(solution)/shard_map/all_to_all | solution.py:67
  122.8 23.3 %copy-start.8 = (u32[32]{0:T(128)S(1)}, u32[32]{0:T(128)}, u32[]{:S(2)}) copy-start(u32[32]{0:T(128)} %constant.25) | copy-start | bytes 388
  139.5 183.3 %all-to-all-start.3 = ((bf16[1,384,8,256]{3,1,0,2:T(8,128)(2,1)}), bf16[1,384,8,256]{3,1,0,2:T(8,128)(2,1)}, u32[]{:S(2)}, u32[]{:S(2)}) async-start(bf16[1,384,8,256]{3,1,0,2:T(8,128)(2,1)} %copy.90), calls=%async_computation.3 | async-start | bytes 3145728 | tf_op jit(solution)/shard_map/all_to_all | solution.py:77
  466.9 4.7 copy-start.1
Sparse Core Ops, SparseCore 0:
  86.3 234.1 all-reduce.2
  322.9 137.0 all-gather.1
where the time goes:
time: 480 us; the launch traced here: 478 us
  waiting for transfers between devices  342 us (71%)
  local copies, waits for them, and re-layouts  48.2 us (10%)
  matrix products  39.4 us (8%)
  starting transfers between devices  19.1 us (4%)
  between operations  14.9 us (3%)
  other arithmetic  14.6 us (3%)
    unnamed x3, waiting for transfers between devices  166 us
    all_gather x1, waiting for transfers between devices, body(): lax.all_gather(stacked, 'dp', axis=1, tiled=True)  137 us
    unnamed x27, local copies, waits for them, and re-layouts  17.9 us
    all_to_all x1, waiting for transfers between devices, body(): lax.all_to_all(route_grad, 'expert', split_axis=1, concat_axis=0, tiled=T...  16.7 us
    mul x1, local copies, waits for them, and re-layouts, body(): jnp.einsum('erc,erd->ced', hidden, scaled, preferred_element_type=jnp.flo...  15.9 us
    all_to_all x1, waiting for transfers between devices, body(): lax.all_to_all(send_scaled, 'expert', split_axis=0, concat_axis=1, tiled=...  12.2 us
    unnamed x2, other arithmetic  11.4 us
    all_to_all x1, waiting for transfers between devices, body(): lax.all_to_all(send_x, 'expert', split_axis=0, concat_axis=1, tiled=True)  9.95 us
  transfers between devices with their start and end apart: 6, of which 5 were waited for; matrix products, arithmetic and copies ran while one was open for 13% of the time, Pallas kernels for 0%

commit v1 on v0

--- a/solution.py
+++ b/solution.py
@@ -2,6 +2,22 @@
 import jax.numpy as jnp
 from jax import lax
 from jax.sharding import PartitionSpec as P
+
+
+def ring_product(shard, axis, dim, contribution):
+    size, index, rows = (lax.axis_size(axis), lax.axis_index(axis), shard.shape[dim])
+    forward = [(i, (i + 1) % size) for i in range(size)]
+    left = [(i, (i - 1) % size) for i in range(size)]
+    middle = size // 2
+    from_left = from_right = shard
+    subtotal = contribution(shard, index * rows)
+    for hop in range(1, middle + 1):
+        from_left = lax.ppermute(from_left, axis, forward)
+        if hop < size - middle:
+            from_right = lax.ppermute(from_right, axis, left)
+            subtotal = subtotal + contribution(from_right, (index + hop) % size * rows)
+        subtotal = subtotal + contribution(from_left, (index - hop) % size * rows)
+    return subtotal
 
 
 def forward_part(rows_x, w_gate, w_up):
@@ -77,11 +93,16 @@
     columns = lax.all_to_all(split_rows, "dp", split_axis=2, concat_axis=1, tiled=True)
     columns = columns.reshape(local_count, -1, feature_rows)
     reduced = (
-        jnp.einsum(
-            "erc,erj->cej",
-            columns,
-            lax.all_gather(stacked, "dp", axis=1, tiled=True),
-            preferred_element_type=jnp.float32,
+        ring_product(
+            stacked,
+            "dp",
+            1,
+            lambda part, offset: jnp.einsum(
+                "erc,erj->cej",
+                lax.dynamic_slice_in_dim(columns, offset, part.shape[1], axis=1),
+                part,
+                preferred_element_type=jnp.float32,
+            ),
         )
         * inverse
     )

time: 480 us -> 481 us (level)
  waiting for transfers between devices: 342 us -> 319 us
  starting transfers between devices: 19.1 us -> 36.9 us
  matrix products: 39.4 us -> 44.8 us
    ppermute x0 -> x7, waiting for transfers between devices: none -> 229 us  [the longest x4 229 us: ring_product(): from_left = lax.ppermute(from_left, axis, forward)]
    all_gather x1 -> x0, waiting for transfers between devices: 137 us -> none  [body(): lax.all_gather(stacked, 'dp', axis=1, tiled=True)]
    unnamed x3 -> x2, waiting for transfers between devices: 166 us -> 67.5 us
    ppermute x0 -> x7, starting transfers between devices: none -> 17.6 us  [the longest x3 10.5 us: ring_product(): from_right = lax.ppermute(from_right, axis, left)]
    all_to_all x1, waiting for transfers between devices: 16.7 us -> 0.01 us  [body(): lax.all_to_all(route_grad, 'expert', split_axis=1, concat_axis=0, tiled=T...]
    dot_general x1 -> x8, matrix products: 5.71 us -> 12.9 us  [body(): jnp.einsum('erc,erj->cej', lax.dynamic_slice_in_dim(columns, offset, part...]
    unnamed x27 -> x35, local copies, waits for them, and re-layouts: 17.9 us -> 18.8 us
  transfers between devices with their start and end apart: 6 -> 12, of which waited for: 5 -> 7; matrix products, arithmetic and copies ran while one was open for 13% -> 15% of each run, Pallas kernels for 0% -> 0%
where the time goes in v1:
time: 481 us; the launch traced here: 479 us
  waiting for transfers between devices  319 us (66%)
  local copies, waits for them, and re-layouts  49 us (10%)
  matrix products  44.8 us (9%)
  starting transfers between devices  36.9 us (8%)
  between operations  15 us (3%)
  other arithmetic  14.7 us (3%)
    ppermute x4, waiting for transfers between devices, ring_product(): from_left = lax.ppermute(from_left, axis, forward)  229 us
    unnamed x2, waiting for transfers between devices  67.5 us
    unnamed x35, local copies, waits for them, and re-layouts  18.8 us
    mul x1, local copies, waits for them, and re-layouts, body(): jnp.einsum('erc,erd->ced', hidden, scaled, preferred_element_type=jnp.flo...  16 us
    dot_general x8, matrix products, body(): jnp.einsum('erc,erj->cej', lax.dynamic_slice_in_dim(columns, offset, part...  12.9 us
    all_to_all x1, waiting for transfers between devices, body(): lax.all_to_all(send_scaled, 'expert', split_axis=0, concat_axis=1, tiled=...  12.1 us
    unnamed x2, other arithmetic  11.3 us
    ppermute x3, starting transfers between devices, ring_product(): from_right = lax.ppermute(from_right, axis, left)  10.5 us
  transfers between devices with their start and end apart: 12, of which 7 were waited for; matrix products, arithmetic and copies ran while one was open for 15% of the time, Pallas kernels for 0%

profile of v1, /device:TPU:0, one launch (start us, length us, event | category | flops | bytes accessed | tf_op | source)
XLA Modules:
  0.0 479.1 jit_solution(14544963493512185925)
XLA Ops:
  7.2 0.9 copy.83
  8.1 0.1 eq.79
  8.3 0.1 eq.75
  8.4 1.2 reduce-window.6
  9.7 0.1 copy.85
  10.1 0.1 reduce_sum.33
  10.3 0.7 multiply_add_fusion.1
  11.0 0.1 fusion.42
  11.1 2.8 convolution_convert_fusion
  13.9 4.4 all-to-all-start.1
  18.3 3.4 mul.113
  21.7 3.7 mul.114
  25.4 0.1 copy.88
  25.5 0.1 mul.111
  25.6 3.5 convolution_convert_fusion.1
  29.1 9.9 %all-to-all-done.1 = bf16[4,96,2048]{2,1,0:T(8,128)(2,1)} async-done(((bf16[4,96,2048]{2,1,0:T(8,128)(2,1)}), bf16[4,96,2048]{2,1,0:T(8,128)(2,1)}, u32[]{:S(2)}, u32[]{:S(2)}) %all-to-all-start.1) | async-done | bytes 1572896 | tf_op jit(solution)/shard_map/all_to_all | solution.py:78
  39.0 4.5 all-to-all-start
  43.6 4.0 fusion.2
  47.6 3.8 fusion.6
  51.4 12.1 %all-to-all-done = bf16[4,96,2048]{2,1,0:T(8,128)(2,1)} async-done(((bf16[4,96,2048]{2,1,0:T(8,128)(2,1)}), bf16[4,96,2048]{2,1,0:T(8,128)(2,1)}, u32[]{:S(2)}, u32[]{:S(2)}) %all-to-all-start) | async-done | bytes 1572896 | tf_op jit(solution)/shard_map/all_to_all | solution.py:79
  63.5 4.7 multiply_convert_fusion.2
  68.3 1.4 fusion
  69.7 0.9 copy-done.10
  70.6 1.4 fusion.16
  72.0 2.4 copy.106
  74.4 0.5 broadcast.82
  74.9 11.2 %reduce.1 = bf16[384,2048]{1,0:T(8,128)(2,1)} reduce(bf16[384,1,2048]{2,1,0:T(2,128)(2,1)S(1)} %bitcast.138, bf16[]{:T(256)} %broadcast.82), dimensions={1}, to_apply=%bitcast.137.reduce_sub_computation | reduce | bytes 3145730
  86.2 4.1 reshape.252
  90.3 3.7 all-to-all-start.2
  94.1 6.3 %multiply_bitcast_fusion = f32[768,1,2048]{0,2,1:T(8,128)} fusion(bf16[384,2048]{1,0:T(8,128)(2,1)} %bitcast.4, f32[384,768]{1,0:T(8,128)} %fusion.6, f32[384,768]{1,0:T(8,128)S(1)} %copy-done.12), kind=kOutput, calls=%fused_computation | convolution fusion | flops 1211301888 | bytes 10223616 | tf_op jit(solution)/shard_map/erc,erd->ced/dot_general | solution.py:112
  100.4 16.0 %copy.91 = f32[768,1,2048]{2,1,0:T(1,128)} copy(f32[768,1,2048]{0,2,1:T(8,128)} %multiply_bitcast_fusion) | data formatting | bytes 12582912 | tf_op jit(solution)/shard_map/mul | solution.py:112
  116.4 1.9 copy.97
  118.3 1.5 copy.90
  119.7 6.6 %all-to-all-start.3 = ((bf16[1,384,8,256]{3,1,0,2:T(8,128)(2,1)}), bf16[1,384,8,256]{3,1,0,2:T(8,128)(2,1)S(1)}, u32[]{:S(2)}, u32[]{:S(2)}) async-start(bf16[1,384,8,256]{3,1,0,2:T(8,128)(2,1)} %copy.90), calls=%async_computation.3 | async-start | bytes 3145728 | tf_op jit(solution)/shard_map/all_to_all | solution.py:93
  126.4 1.3 pad_maximum_fusion
  127.7 2.1 collective-permute-start.1
  129.8 2.8 collective-permute-start
  132.5 101.1 %collective-permute-done.1 = bf16[1,384,1536]{2,1,0:T(8,128)(2,1)S(1)} collective-permute-done((bf16[1,384,1536]{2,1,0:T(8,128)(2,1)S(1)}, bf16[1,384,1536]{2,1,0:T(8,128)(2,1)S(1)}, u32[]{:S(2)}, u32[]{:S(2)}) %collective-permute-start.1) | collective-permute-done | bytes 1179680 | tf_op jit(solution)/shard_map/ppermute | solution.py:15
  233.6 1.0 copy-done.4
  234.7 4.7 collective-permute-start.2
  239.4 45.5 %collective-permute-done.3 = bf16[1,384,1536]{2,1,0:T(8,128)(2,1)} collective-permute-done((bf16[1,384,1536]{2,1,0:T(8,128)(2,1)S(1)}, bf16[1,384,1536]{2,1,0:T(8,128)(2,1)}, u32[]{:S(2)}, u32[]{:S(2)}) %collective-permute-start.3) | collective-permute-done | bytes 1179680 | tf_op jit(solution)/shard_map/ppermute | solution.py:15
  284.9 2.6 collective-permute-start.5
  287.5 0.6 dynamic-slice
  288.7 2.9 reshape.253
  291.6 4.0 fusion.22
  295.6 3.0 collective-permute-start.4
  298.6 1.2 copy-done.2
  299.8 1.9 fusion.34
  301.6 2.0 convolution_add_fusion.4
  303.8 0.6 convolution_add_fusion.3
  304.4 44.0 %collective-permute-done.5 = bf16[1,384,1536]{2,1,0:T(8,128)(2,1)} collective-permute-done((bf16[1,384,1536]{2,1,0:T(8,128)(2,1)}, bf16[1,384,1536]{2,1,0:T(8,128)(2,1)}, u32[]{:S(2)}, u32[]{:S(2)}) %collective-permute-start.5) | collective-permute-done | bytes 1179680 | tf_op jit(solution)/shard_map/ppermute | solution.py:15
  348.4 2.5 collective-permute-start.6
  350.9 1.9 fusion.29
  352.8 2.0 fusion.14
  354.8 1.9 fusion.26
  356.7 2.0 fusion.13
  358.7 38.5 %collective-permute-done.6 = bf16[1,384,1536]{2,1,0:T(8,128)(2,1)S(1)} collective-permute-done((bf16[1,384,1536]{2,1,0:T(8,128)(2,1)}, bf16[1,384,1536]{2,1,0:T(8,128)(2,1)S(1)}, u32[]{:S(2)}, u32[]{:S(2)}) %collective-permute-start.6) | collective-permute-done | bytes 1179680 | tf_op jit(solution)/shard_map/ppermute | solution.py:15
  397.2 0.6 fusion.15
  397.9 1.0 slice_bitcast_fusion
  398.8 1.1 copy.92
  400.0 2.5 copy.93
  402.4 67.5 %all-reduce.3.cloned.1.call-done = f32[768,1,2048]{2,1,0:T(1,128)} async-done(((f32[768,1,2048]{2,1,0:T(1,128)}), f32[768,1,2048]{2,1,0:T(1,128)}) %all-reduce.3.cloned.1.call-update) | async-done | bytes 6291472
  470.0 1.2 dynamic-slice_bitcast_fusion
  471.1 1.1 copy.94
  (41 shorter events, 0.6 us)
Async XLA Ops:
  7.2 36.4 %copy-start = (bf16[1,2048,768]{2,1,0:T(8,128)(2,1)S(1)}, bf16[1,2048,768]{2,1,0:T(8,128)(2,1)}, u32[]{:S(2)}) copy-start(bf16[1,2048,768]{2,1,0:T(8,128)(2,1)} %param.11) | copy-start | bytes 9437188
  13.9 25.1 %all-to-all-start.1 = ((bf16[4,96,2048]{2,1,0:T(8,128)(2,1)}), bf16[4,96,2048]{2,1,0:T(8,128)(2,1)}, u32[]{:S(2)}, u32[]{:S(2)}) async-start(bf16[4,96,2048]{2,1,0:T(8,128)(2,1)} %bitcast.139), calls=%async_computation.1 | async-start | bytes 3145728 | tf_op jit(solution)/shard_map/all_to_all | solution.py:78
  21.7 3.7 copy-start.8
  39.0 24.5 %all-to-all-start = ((bf16[4,96,2048]{2,1,0:T(8,128)(2,1)}), bf16[4,96,2048]{2,1,0:T(8,128)(2,1)}, u32[]{:S(2)}, u32[]{:S(2)}) async-start(bf16[4,96,2048]{2,1,0:T(8,128)(2,1)} %bitcast.140), calls=%async_computation | async-start | bytes 3145728 | tf_op jit(solution)/shard_map/all_to_all | solution.py:79
  43.6 4.0 copy-start.9
  68.2 1.5 copy-start.7
  68.2 1.5 copy-start.6
  68.2 2.3 copy-start.10
  90.3 3.8 copy-start.12
  90.3 29.4 %all-to-all-start.2 = ((bf16[4,2,98304]{2,1,0:T(2,128)(2,1)}), bf16[4,2,98304]{2,1,0:T(2,128)(2,1)S(1)}, u32[]{:S(2)}, u32[]{:S(2)}) async-start(bf16[4,2,98304]{2,1,0:T(2,128)(2,1)} %reshape.252), calls=%async_computation.2 | async-start | bytes 3145728 | tf_op jit(solution)/shard_map/all_to_all | solution.py:83
  94.0 376.0 %all-reduce.3.cloned.1.call-start = ((), (), s32[]{:S(2)}) async-start(), calls=%async_computation.4 | async-start | bytes 12582912
  119.7 178.9 %all-to-all-start.3 = ((bf16[1,384,8,256]{3,1,0,2:T(8,128)(2,1)}), bf16[1,384,8,256]{3,1,0,2:T(8,128)(2,1)S(1)}, u32[]{:S(2)}, u32[]{:S(2)}) async-start(bf16[1,384,8,256]{3,1,0,2:T(8,128)(2,1)} %copy.90), calls=%async_computation.3 | async-start | bytes 3145728 | tf_op jit(solution)/shard_map/all_to_all | solution.py:93
  126.4 161.1 %copy-start.11 = (u32[32]{0:T(128)S(1)}, u32[32]{0:T(128)}, u32[]{:S(2)}) copy-start(u32[32]{0:T(128)} %constant.86) | copy-start | bytes 388
  127.7 105.9 %collective-permute-start.1 = (bf16[1,384,1536]{2,1,0:T(8,128)(2,1)S(1)}, bf16[1,384,1536]{2,1,0:T(8,128)(2,1)S(1)}, u32[]{:S(2)}, u32[]{:S(2)}) collective-permute-start(bf16[1,384,1536]{2,1,0:T(8,128)(2,1)S(1)} %pad_maximum_fusion), channel_id=1, source_target_pairs={{0,4},{4,8},{8,12},{12,16},{16,20},{20,24},{24,28},{28,0},{1,5},{5... | collective-permute-start | bytes 3538952 | tf_op jit(solution)/shard_map/ppermute | solution.py:15
  129.8 104.9 %collective-permute-start = (bf16[1,384,1536]{2,1,0:T(8,128)(2,1)S(1)}, bf16[1,384,1536]{2,1,0:T(8,128)(2,1)}, u32[]{:S(2)}, u32[]{:S(2)}) collective-permute-start(bf16[1,384,1536]{2,1,0:T(8,128)(2,1)S(1)} %pad_maximum_fusion), channel_id=1, source_target_pairs={{0,28},{4,0},{8,4},{12,8},{16,12},{20,16},{24,20},{28,24},{1,29},{... | collective-permute-start | bytes 3538952 | tf_op jit(solution)/shard_map/ppermute | solution.py:17
  233.6 1.0 copy-start.4
  234.7 50.3 %collective-permute-start.3 = (bf16[1,384,1536]{2,1,0:T(8,128)(2,1)S(1)}, bf16[1,384,1536]{2,1,0:T(8,128)(2,1)}, u32[]{:S(2)}, u32[]{:S(2)}) collective-permute-start(bf16[1,384,1536]{2,1,0:T(8,128)(2,1)S(1)} %collective-permute-done.1), channel_id=1, source_target_pairs={{0,4},{4,8},{8,12},{12,16},{16,20},{20,24},{24,28},{28,0},{1,5},{5... | collective-permute-start | bytes 3538952 | tf_op jit(solution)/shard_map/ppermute | solution.py:15
  234.7 61.0 %collective-permute-start.2 = (bf16[1,384,1536]{2,1,0:T(8,128)(2,1)}, bf16[1,384,1536]{2,1,0:T(8,128)(2,1)}, u32[]{:S(2)}, u32[]{:S(2)}) collective-permute-start(bf16[1,384,1536]{2,1,0:T(8,128)(2,1)} %collective-permute-done), channel_id=1, source_target_pairs={{0,28},{4,0},{8,4},{12,8},{16,12},{20,16},{24,20},{28,24},{1,29},{... | collective-permute-start | bytes 3538952 | tf_op jit(solution)/shard_map/ppermute | solution.py:17
  284.9 63.5 %collective-permute-start.5 = (bf16[1,384,1536]{2,1,0:T(8,128)(2,1)}, bf16[1,384,1536]{2,1,0:T(8,128)(2,1)}, u32[]{:S(2)}, u32[]{:S(2)}) collective-permute-start(bf16[1,384,1536]{2,1,0:T(8,128)(2,1)} %collective-permute-done.3), channel_id=1, source_target_pairs={{0,4},{4,8},{8,12},{12,16},{16,20},{20,24},{24,28},{28,0},{1,5},{5... | collective-permute-start | bytes 3538952 | tf_op jit(solution)/shard_map/ppermute | solution.py:15
  295.6 61.1 %collective-permute-start.4 = (bf16[1,384,1536]{2,1,0:T(8,128)(2,1)}, bf16[1,384,1536]{2,1,0:T(8,128)(2,1)}, u32[]{:S(2)}, u32[]{:S(2)}) collective-permute-start(bf16[1,384,1536]{2,1,0:T(8,128)(2,1)} %collective-permute-done.2), channel_id=1, source_target_pairs={{0,28},{4,0},{8,4},{12,8},{16,12},{20,16},{24,20},{28,24},{1,29},{... | collective-permute-start | bytes 3538952 | tf_op jit(solution)/shard_map/ppermute | solution.py:17
  298.6 1.2 copy-start.2
  301.6 2.1 copy-start.3
  301.6 2.1 copy-start.5
  348.4 48.8 %collective-permute-start.6 = (bf16[1,384,1536]{2,1,0:T(8,128)(2,1)}, bf16[1,384,1536]{2,1,0:T(8,128)(2,1)S(1)}, u32[]{:S(2)}, u32[]{:S(2)}) collective-permute-start(bf16[1,384,1536]{2,1,0:T(8,128)(2,1)} %collective-permute-done.5), channel_id=1, source_target_pairs={{0,4},{4,8},{8,12},{12,16},{16,20},{20,24},{24,28},{28,0},{1,5},{5... | collective-permute-start | bytes 3538952 | tf_op jit(solution)/shard_map/ppermute | solution.py:15
  400.0 72.3 %copy-start.1 = (bf16[1,2048,768]{2,1,0:T(8,128)(2,1)S(1)}, bf16[1,2048,768]{2,1,0:T(8,128)(2,1)}, u32[]{:S(2)}) copy-start(bf16[1,2048,768]{2,1,0:T(8,128)(2,1)} %param.11) | copy-start | bytes 9437188
Sparse Core Ops, SparseCore 0:
  116.5 353.4 all-reduce.2
